TPU v7x, 32 devices: a whole 2x2x4 slice. The times are simulated.
32 devices in a mesh: gx: 8 (over y, x, core), pa: 4 (over z).
Axes of the slice: x: 2, y: 2, z: 4, core: 2. Of those that a mesh axis runs over, the one named last changes fastest.
Arguments:
- block_inverses: float32 [32, 32, 128, 128], P('gx', 'pa'), parts along dimension 1, may hold values from -0.25 to 1.07, as said below
- residual: float32 [32, 32, 128], P('gx', 'pa'), parts along dimension 1, may hold values from -0.3 to 0.3
- material: int32 [32, 32, 128], P('gx', 'pa'), parts along dimension 1, may hold values from 0 to 3
- fin_mask: int32 [32, 32, 128], P('gx', 'pa'), parts along dimension 1, may hold values 0 or 1
- phase_mask: int32 [32, 32, 128], P('gx', 'pa'), parts along dimension 1, may hold values 0 or 1
- k_table: float32 [4], replicated, may hold values from 0.95 to 1.05
Outputs:
- correction: float32 [32, 32, 128], P('gx', 'pa'), parts along dimension 1
- enthalpy_step: float32 [32, 32, 128], P('gx', 'pa'), parts along dimension 1
There are 4 independent parts, one for each index of `pa`. A program takes and returns all parts, laid end to end along the dimension named above; an argument that names none is the same for every part. Nothing has to cross between parts.
Inputs may be any that keep to these rules, and one draw needn't show every extreme that they name: Each block block_inverses[i, t] is a symmetric matrix.
All inputs are finite; a program needn't handle non-finite values. No bound on the sum of `fin_mask` or of `phase_mask` on one device may be relied on, other than what follows from the above.
Results may differ from a plain program's by a relative error of at most 0.0003.
Values sent between devices are 32-bit elements; how exact they have to be, the bound alone decides.
No kernel may reach another device: no remote copies, remote signals or barrier semaphores. Data moves between devices by JAX's collectives and lax.ppermute only.
A program may use at most 128 MiB of HBM per device.

v0:
```python
import jax
import jax.numpy as jnp
from jax import lax
from jax.sharding import PartitionSpec as P


def passed_along(block, axis, distance):
    devices = range(lax.axis_size(axis))
    route = [(i - distance, i) for i in devices if i - distance in devices]
    return lax.ppermute(block, axis, route)


def apply_block(pivot_entries, vector):
    return jnp.einsum("tab,tb->ta", pivot_entries, vector, precision=lax.Precision.HIGHEST)


def apply_transposed(pivot_entries, vector):
    return jnp.einsum("tba,tb->ta", pivot_entries, vector, precision=lax.Precision.HIGHEST)


def forward_pass(block_inverses, residual, face_cond, entering):
    state_vec = entering
    results = []
    for line_position in range(block_inverses.shape[0]):
        state_vec = apply_block(
            block_inverses[line_position],
            residual[line_position] + face_cond[line_position] * state_vec,
        )
        results.append(state_vec)
    return jnp.stack(results)


def backward_pass(block_inverses, forward_vals, face_cond, arriving):
    carried = arriving
    results = [None] * block_inverses.shape[0]
    for line_position in reversed(range(block_inverses.shape[0])):
        solved = forward_vals[line_position] + apply_block(block_inverses[line_position], carried)
        results[line_position] = solved
        carried = face_cond[line_position] * solved
    return (jnp.stack(results), carried)


def on_device(block_inverses, residual, material, fin_mask, phase_mask, k_table):
    block_count, tile_count, cell_count = residual.shape
    material_codes = jnp.arange(k_table.shape[0], dtype=jnp.int32)
    conduct = jnp.sum(
        jnp.where(material[..., None] == material_codes, k_table, jnp.zeros_like(k_table)), axis=-1
    )
    before = passed_along(conduct[block_count - 1], "gx", 1)
    earlier = jnp.concatenate([before[None], conduct[: block_count - 1]], axis=0)
    face_cond = (
        2.0 * conduct * earlier / (conduct + earlier) * (0.9 + 0.1 * fin_mask.astype(jnp.float32))
    )
    zero_vector = jnp.zeros((tile_count, cell_count), jnp.float32)
    scaled_rows = block_inverses * face_cond[:, :, None, :]
    matrix_product = scaled_rows[0]
    for line_position in range(1, block_count):
        matrix_product = jnp.einsum(
            "hzp,hpn->hzn",
            scaled_rows[line_position],
            matrix_product,
            precision=lax.Precision.HIGHEST,
        )
    local_vals = forward_pass(block_inverses, residual, face_cond, zero_vector)
    tail_vec = local_vals[block_count - 1]
    all_maps, all_tails = (
        lax.all_gather(matrix_product[None], "gx", axis=0, tiled=True),
        lax.all_gather(tail_vec[None], "gx", axis=0, tiled=True),
    )
    own_index = lax.axis_index("gx")
    processor_total = all_maps.shape[0]

    def fold_forward(line_position, state_vec):
        moved = apply_block(all_maps[line_position], state_vec) + all_tails[line_position]
        return jnp.where(line_position < own_index, moved, state_vec)

    entering = lax.fori_loop(0, processor_total, fold_forward, zero_vector, unroll=8)
    forward_vals = forward_pass(block_inverses, residual, face_cond, entering)
    _, leaving = backward_pass(block_inverses, forward_vals, face_cond, zero_vector)
    all_leaving = lax.all_gather(leaving[None], "gx", axis=0, tiled=True)

    def backward_accumulate(offset, state_vec):
        line_position = processor_total - 1 - offset
        moved = apply_transposed(all_maps[line_position], state_vec) + all_leaving[line_position]
        return jnp.where(line_position > own_index, moved, state_vec)

    arriving = lax.fori_loop(0, processor_total, backward_accumulate, zero_vector, unroll=8)
    correction, _ = backward_pass(block_inverses, forward_vals, face_cond, arriving)
    enthalpy_step = correction * (1.0 + 2.0 * phase_mask.astype(jnp.float32))
    return (correction, enthalpy_step)


def solution(mesh):
    return jax.shard_map(
        on_device,
        mesh=mesh,
        in_specs=(
            P("gx", "pa", None, None),
            P("gx", "pa", None),
            P("gx", "pa", None),
            P("gx", "pa", None),
            P("gx", "pa", None),
            P(),
        ),
        out_specs=(P("gx", "pa", None), P("gx", "pa", None)),
        check_vma=False,
    )
```

profile of v0, /device:TPU:0, one launch (start us, length us, event | category | flops | bytes accessed | tf_op | source)
XLA Modules:
  0.0 100.5 jit_solution(474527091113292094)
XLA Ops:
  7.2 0.8 select_reduce_fusion
  8.0 2.3 %collective-permute-start = (f32[8,128]{1,0:T(8,128)S(1)}, f32[8,128]{1,0:T(8,128)S(1)}, u32[]{:S(2)}, u32[]{:S(2)}) collective-permute-start(f32[8,128]{1,0:T(8,128)S(1)} %slice_bitcast_fusion.12), channel_id=1, source_target_pairs={{0,4},{4,8},{8,12},{12,16},{16,20},{20,24},{24,28},{1,5},{5,9},{9,... | collective-permute-start | bytes 12296 | tf_op jit(solution)/shard_map/ppermute | solution.py:10
  10.4 0.8 collective-permute-done
  11.9 1.9 %broadcast_multiply_fusion = f32[4,8,128,128]{3,2,1,0:T(8,128)S(1)} fusion(f32[4,8,128,128]{3,2,1,0:T(8,128)} %param.6, f32[4,8,128]{2,1,0:T(8,128)S(1)} %add_multiply_fusion.1), kind=kLoop, calls=%fused_computation | loop fusion | flops 524288 | bytes 4210688 | tf_op jit(solution)/shard_map/mul | solution.py:55
  15.2 1.5 %fusion.2 = f32[8,128,128]{2,1,0:T(8,128)} fusion(f32[8,128,128]{2,1,0:T(8,128)S(1)} %fusion.1, f32[4,8,128,128]{3,2,1,0:T(8,128)S(1)} %broadcast_multiply_fusion), kind=kOutput, calls=%fused_computation.7 | convolution fusion | flops 201326592 | bytes 1572864 | tf_op jit(solution)/shard_map/hzp,hpn->hzn/dot_general | solution.py:58
  16.8 0.9 fusion.5
  17.7 0.9 fusion.33
  18.6 0.9 fusion.25
  19.6 1.0 fusion.17
  20.5 0.9 fusion.9
  21.5 13.4 %all-gather.1 = f32[64,128]{1,0:T(8,128)S(1)} all-gather(f32[8,128]{1,0:T(8,128)S(1)} %bitcast.349), channel_id=3, replica_groups=mesh['gx'=8,'pa'=4] {'gx'}, dimensions={0}, use_global_device_ids=true | all-gather | bytes 36864 | tf_op jit(solution)/shard_map/all_gather | solution.py:68
  34.8 23.2 %all-gather.5.cloned.1.call-done = f32[64,128,128]{2,1,0:T(8,128)} async-done(((f32[8,128,128]{2,1,0:T(8,128)}), f32[64,128,128]{2,1,0:T(8,128)}) %all-gather.5.cloned.1.call-update) | async-done | bytes 4194320 | tf_op jit(solution)/shard_map/all_gather | solution.py:67
  58.0 2.1 %fusion.72 = f32[8,1,128]{2,1,0:T(1,128)S(1)} fusion(f32[64,128,128]{2,1,0:T(8,128)} %all-gather.5.cloned.1.call-done, f32[8,128,1]{1,2,0:T(1,128)S(1)} %bitcast.312), kind=kOutput, calls=%fused_computation.119 | convolution fusion | flops 1572864 | bytes 4202496 | tf_op jit(solution)/shard_map/eval_jaxpr/tab,tb->ta/dot_general | solution.py:14
  60.1 2.0 %fusion.73 = f32[8,1,128]{2,1,0:T(1,128)S(1)} fusion(f32[64,128,128]{2,1,0:T(8,128)} %all-gather.5.cloned.1.call-done, f32[8,128,1]{1,2,0:T(1,128)S(1)} %bitcast.326), kind=kOutput, calls=%fused_computation.120 | convolution fusion | flops 1572864 | bytes 4202496 | tf_op jit(solution)/shard_map/eval_jaxpr/tab,tb->ta/dot_general | solution.py:14
  62.1 2.0 %fusion.74 = f32[8,1,128]{2,1,0:T(1,128)S(1)} fusion(f32[64,128,128]{2,1,0:T(8,128)} %all-gather.5.cloned.1.call-done, f32[8,128,1]{1,2,0:T(1,128)S(1)} %bitcast.329), kind=kOutput, calls=%fused_computation.121 | convolution fusion | flops 1572864 | bytes 4202496 | tf_op jit(solution)/shard_map/eval_jaxpr/tab,tb->ta/dot_general | solution.py:14
  64.1 0.9 fusion.75
  65.0 0.9 fusion.76
  66.0 0.9 fusion.77
  66.9 0.9 fusion.78
  67.9 0.9 fusion.79
  68.8 0.9 fusion.31
  69.7 0.9 fusion.23
  70.7 0.9 fusion.15
  71.6 0.9 fusion.7
  72.6 0.9 fusion.13
  73.5 0.9 fusion.21
  74.5 0.9 fusion.29
  75.4 9.2 %all-gather.2 = f32[64,128]{1,0:T(8,128)S(1)} all-gather(f32[8,128]{1,0:T(8,128)S(1)} %add_multiply_fusion.2), channel_id=4, replica_groups=mesh['gx'=8,'pa'=4] {'gx'}, dimensions={0}, use_global_device_ids=true | all-gather | bytes 36864 | tf_op jit(solution)/shard_map/all_gather | solution.py:80
  89.2 0.9 fusion.3
  90.2 0.9 fusion.11
  91.1 0.9 fusion.19
  92.0 0.9 fusion.27
  (56 shorter events, 7.5 us)
Async XLA Ops:
  7.2 50.9 %all-gather.5.cloned.1.call-start = ((), (), s32[]{:S(2)}) async-start(), calls=%async_computation | async-start | bytes 4718592 | tf_op jit(solution)/shard_map/all_gather | solution.py:67
  8.0 3.2 %collective-permute-start = (f32[8,128]{1,0:T(8,128)S(1)}, f32[8,128]{1,0:T(8,128)S(1)}, u32[]{:S(2)}, u32[]{:S(2)}) collective-permute-start(f32[8,128]{1,0:T(8,128)S(1)} %slice_bitcast_fusion.12), channel_id=1, source_target_pairs={{0,4},{4,8},{8,12},{12,16},{16,20},{20,24},{24,28},{1,5},{5,9},{9,... | collective-permute-start | bytes 12296 | tf_op jit(solution)/shard_map/ppermute | solution.py:10
  11.9 4.8 %copy-start.1 = (f32[4,8,128,128]{3,2,1,0:T(8,128)S(1)}, f32[4,8,128,128]{3,2,1,0:T(8,128)}, u32[]{:S(2)}) copy-start(f32[4,8,128,128]{3,2,1,0:T(8,128)} %param.6) | copy-start | bytes 6291460
  11.9 5.8 %copy-start.2 = (f32[4,8,128]{2,1,0:T(8,128)S(1)}, f32[4,8,128]{2,1,0:T(8,128)}, u32[]{:S(2)}) copy-start(f32[4,8,128]{2,1,0:T(8,128)} %param.7) | copy-start | bytes 49156
  58.0 6.1 %copy-start = (f32[64,128,128]{2,1,0:T(8,128)S(1)}, f32[64,128,128]{2,1,0:T(8,128)}, u32[]{:S(2)}) copy-start(f32[64,128,128]{2,1,0:T(8,128)} %all-gather.5.cloned.1.call-done) | copy-start | bytes 12582916
  86.9 6.1 %copy-start.3 = (s32[4,8,128]{2,1,0:T(8,128)S(1)}, s32[4,8,128]{2,1,0:T(8,128)}, u32[]{:S(2)}) copy-start(s32[4,8,128]{2,1,0:T(8,128)} %param.10) | copy-start | bytes 49156
Sparse Core Ops, SparseCore 0:
  16.8 41.1 all-gather.4
where the time goes:
time: 101 us; the launch traced here: 100 us
  matrix products  32.9 us (33%)
  waiting for transfers between devices  24 us (24%)
  blocking collectives  22.6 us (22%)
  between operations  14.2 us (14%)
  other arithmetic  4.31 us (4%)
  starting transfers between devices  2.38 us (2%)
    dot_general x24, matrix products, apply_block(): jnp.einsum('tab,tb->ta', pivot_entries, vector, precision=lax.Precision.H...  25.7 us
    all_gather x1, waiting for transfers between devices, on_device(): lax.all_gather(matrix_product[None], 'gx', axis=0, tiled=True)  23.2 us
    all_gather x1, blocking collectives, on_device(): lax.all_gather(tail_vec[None], 'gx', axis=0, tiled=True)  13.4 us
    all_gather x1, blocking collectives, on_device(): all_leaving = lax.all_gather(leaving[None], 'gx', axis=0, tiled=True)  9.25 us
    dot_general x8, matrix products, apply_transposed(): jnp.einsum('tba,tb->ta', pivot_entries, vector, precision=lax.Precision.H...  4.48 us
    dot_general x3, matrix products, on_device(): jnp.einsum('hzp,hpn->hzn', scaled_rows[line_position], matrix_product, pr...  2.81 us
    ppermute x1, starting transfers between devices, passed_along(): return lax.ppermute(block, axis, route)  2.35 us
  transfers between devices with their start and end apart: 2, of which 2 were waited for; matrix products, arithmetic and copies ran while one was open for 5% of the time, Pallas kernels for 0%

commit v1 on v0

--- a/solution.py
+++ b/solution.py
@@ -1,7 +1,23 @@
+import functools
 import jax
 import jax.numpy as jnp
 from jax import lax
 from jax.sharding import PartitionSpec as P
+
+
+def manage_keys(vec, axis_id):
+    known, b_now = (lax.axis_size(axis_id), lax.axis_index(axis_id))
+    reached, now = (vec, 1)
+    while now < known:
+        main = lax.ppermute(reached, axis_id, tuple(((j, j ^ now) for j in range(known))))
+        tile_out = jnp.concatenate([reached, main], axis=0)
+        w2 = jnp.concatenate([main, reached], axis=0)
+        reached = jnp.where(b_now & now == 0, tile_out, w2)
+        now = 2 * now
+    return reached
+
+
+proceed_wall = functools.partial(manage_keys, axis_id="gx")
 
 
 def passed_along(block, axis, distance):
@@ -64,7 +80,7 @@
     local_vals = forward_pass(block_inverses, residual, face_cond, zero_vector)
     tail_vec = local_vals[block_count - 1]
     all_maps, all_tails = (
-        lax.all_gather(matrix_product[None], "gx", axis=0, tiled=True),
+        proceed_wall(matrix_product[None]),
         lax.all_gather(tail_vec[None], "gx", axis=0, tiled=True),
     )
     own_index = lax.axis_index("gx")

time: 101 us -> 131 us (1.30)
  blocking collectives: 22.6 us -> 53.5 us
  between operations: 14.2 us -> 0.74 us
  starting transfers between devices: 2.38 us -> 10.2 us
  other arithmetic: 4.31 us -> 11.6 us
  matrix products: 32.9 us -> 28.9 us
  waiting for transfers between devices: 24 us -> 25.9 us
    all_gather x1, blocking collectives: 13.4 us -> 44.2 us  [on_device(): lax.all_gather(tail_vec[None], 'gx', axis=0, tiled=True)]
    ppermute x0 -> x3, waiting for transfers between devices: none -> 25.1 us  [manage_keys(): lax.ppermute(reached, axis_id, tuple(((j, j ^ now) for j in range(known))))]
    all_gather x1 -> x0, waiting for transfers between devices: 23.2 us -> none  [on_device(): lax.all_gather(matrix_product[None], 'gx', axis=0, tiled=True)]
    ppermute x0 -> x3, starting transfers between devices: none -> 7.86 us  [manage_keys(): lax.ppermute(reached, axis_id, tuple(((j, j ^ now) for j in range(known))))]
    select_n x0 -> x3, other arithmetic: none -> 7.42 us  [manage_keys(): reached = jnp.where(b_now & now == 0, tile_out, w2)]
    dot_general x24, matrix products: 25.7 us -> 22.4 us  [apply_block(): jnp.einsum('tab,tb->ta', pivot_entries, vector, precision=lax.Precision.H...]
  transfers between devices with their start and end apart: 2 -> 4, of which waited for: 2 -> 3; matrix products, arithmetic and copies ran while one was open for 5% -> 4% of each run, Pallas kernels for 0% -> 0%
where the time goes in v1:
time: 131 us
  blocking collectives  53.5 us (41%)
  matrix products  28.9 us (22%)
  waiting for transfers between devices  25.9 us (20%)
  other arithmetic  11.6 us (9%)
  starting transfers between devices  10.2 us (8%)
    all_gather x1, blocking collectives, on_device(): lax.all_gather(tail_vec[None], 'gx', axis=0, tiled=True)  44.2 us
    ppermute x3, waiting for transfers between devices, manage_keys(): lax.ppermute(reached, axis_id, tuple(((j, j ^ now) for j in range(known))))  25.1 us
    dot_general x24, matrix products, apply_block(): jnp.einsum('tab,tb->ta', pivot_entries, vector, precision=lax.Precision.H...  22.4 us
    all_gather x1, blocking collectives, on_device(): all_leaving = lax.all_gather(leaving[None], 'gx', axis=0, tiled=True)  9.3 us
    ppermute x3, starting transfers between devices, manage_keys(): lax.ppermute(reached, axis_id, tuple(((j, j ^ now) for j in range(known))))  7.86 us
    select_n x3, other arithmetic, manage_keys(): reached = jnp.where(b_now & now == 0, tile_out, w2)  7.42 us
    dot_general x8, matrix products, apply_transposed(): jnp.einsum('tba,tb->ta', pivot_entries, vector, precision=lax.Precision.H...  4.49 us
  transfers between devices with their start and end apart: 4, of which 3 were waited for; matrix products, arithmetic and copies ran while one was open for 4% of the time, Pallas kernels for 0%

profile of v1, /device:TPU:0, one launch (start us, length us, event | category | flops | bytes accessed | tf_op | source)
XLA Modules:
  0.0 130.8 jit_solution(9764391191305653658)
XLA Ops:
  1.4 2.3 %collective-permute-start = (f32[8,128]{1,0:T(8,128)S(1)}, f32[8,128]{1,0:T(8,128)S(1)}, u32[]{:S(2)}, u32[]{:S(2)}) collective-permute-start(f32[8,128]{1,0:T(8,128)S(1)} %slice_bitcast_fusion.36), channel_id=1, source_target_pairs={{0,4},{4,8},{8,12},{12,16},{16,20},{20,24},{24,28},{1,5},{5,9},{9,... | collective-permute-start | bytes 12296 | tf_op jit(solution)/shard_map/ppermute | solution.py:26
  5.3 1.8 %broadcast_multiply_fusion = f32[4,8,128,128]{3,2,1,0:T(8,128)S(1)} fusion(f32[4,8,128,128]{3,2,1,0:T(8,128)} %param.6, f32[4,8,128]{2,1,0:T(8,128)S(1)} %add_multiply_fusion.1), kind=kLoop, calls=%fused_computation.4 | loop fusion | flops 524288 | bytes 4210688 | tf_op jit(solution)/shard_map/mul | solution.py:71
  9.1 2.6 %collective-permute-start.1 = (f32[1,8,128,128]{3,2,1,0:T(8,128)S(1)}, f32[1,8,128,128]{3,2,1,0:T(8,128)S(1)}, u32[]{:S(2)}, u32[]{:S(2)}) collective-permute-start(f32[1,8,128,128]{3,2,1,0:T(8,128)S(1)} %convolution_bitcast_fusion), channel_id=1, source_target_pairs={{0,4},{4,0},{8,12},{12,8},{16,20},{20,16},{24,28},{28,24},{1,5},{5... | collective-permute-start | bytes 1572872 | tf_op jit(solution)/shard_map/ppermute | solution.py:12
  11.7 1.5 %collective-permute-done.1 = f32[1,8,128,128]{3,2,1,0:T(8,128)S(1)} collective-permute-done((f32[1,8,128,128]{3,2,1,0:T(8,128)S(1)}, f32[1,8,128,128]{3,2,1,0:T(8,128)S(1)}, u32[]{:S(2)}, u32[]{:S(2)}) %collective-permute-start.1) | collective-permute-done | bytes 524320 | tf_op jit(solution)/shard_map/ppermute | solution.py:12
  13.4 2.6 %collective-permute-start.2 = (f32[2,8,128,128]{3,2,1,0:T(8,128)S(1)}, f32[2,8,128,128]{3,2,1,0:T(8,128)}, u32[]{:S(2)}, u32[]{:S(2)}) collective-permute-start(f32[2,8,128,128]{3,2,1,0:T(8,128)S(1)} %maximum_select_fusion.2), channel_id=1, source_target_pairs={{0,8},{4,12},{8,0},{12,4},{16,24},{20,28},{24,16},{28,20},{1,9},{5... | collective-permute-start | bytes 3145736 | tf_op jit(solution)/shard_map/ppermute | solution.py:12
  16.0 23.6 %collective-permute-done.2 = f32[2,8,128,128]{3,2,1,0:T(8,128)} collective-permute-done((f32[2,8,128,128]{3,2,1,0:T(8,128)S(1)}, f32[2,8,128,128]{3,2,1,0:T(8,128)}, u32[]{:S(2)}, u32[]{:S(2)}) %collective-permute-start.2) | collective-permute-done | bytes 1048608 | tf_op jit(solution)/shard_map/ppermute | solution.py:12
  39.5 3.1 %maximum_select_fusion.1 = f32[4,8,128,128]{3,2,1,0:T(8,128)} fusion(f32[2,8,128,128]{3,2,1,0:T(8,128)} %collective-permute-done.2, f32[2,8,128,128]{3,2,1,0:T(8,128)S(1)} %maximum_select_fusion.2, pred[]{:T(512)S(6)} %eq.26), kind=kLoop, calls=%fused_computation.1 | loop fusion | flops 1572864 | bytes 4194305 | tf_op jit(solution)/shard_map/jit(_where)/select_n | solution.py:15
  42.6 2.7 %collective-permute-start.3 = (f32[4,8,128,128]{3,2,1,0:T(8,128)}, f32[4,8,128,128]{3,2,1,0:T(8,128)}, u32[]{:S(2)}, u32[]{:S(2)}) collective-permute-start(f32[4,8,128,128]{3,2,1,0:T(8,128)} %maximum_select_fusion.1), channel_id=1, source_target_pairs={{0,16},{4,20},{8,24},{12,28},{16,0},{20,4},{24,8},{28,12},{1,17},{... | collective-permute-start | bytes 6291464 | tf_op jit(solution)/shard_map/ppermute | solution.py:12
  46.2 0.9 fusion.32
  47.2 0.9 fusion.24
  48.1 0.9 fusion.16
  49.1 0.9 fusion.8
  50.0 44.2 %all-gather = f32[64,128]{1,0:T(8,128)S(1)} all-gather(f32[8,128]{1,0:T(8,128)S(1)} %bitcast.368), channel_id=2, replica_groups=mesh['gx'=8,'pa'=4] {'gx'}, dimensions={0}, use_global_device_ids=true | all-gather | bytes 36864 | tf_op jit(solution)/shard_map/all_gather | solution.py:84
  94.2 4.2 %maximum_select_fusion = f32[8,8,128,128]{3,2,1,0:T(8,128)S(1)} fusion(f32[4,8,128,128]{3,2,1,0:T(8,128)} %collective-permute-done.3, f32[4,8,128,128]{3,2,1,0:T(8,128)} %maximum_select_fusion.1, pred[]{:T(512)S(6)} %eq.25), kind=kLoop, calls=%fused_computation | loop fusion | flops 3145728 | bytes 8388609 | tf_op jit(solution)/shard_map/jit(_where)/select_n | solution.py:15
  100.8 0.9 fusion.45
  101.8 0.9 fusion.43
  102.7 0.9 fusion.41
  103.7 0.9 fusion.39
  104.6 0.9 fusion.37
  105.5 0.9 fusion.35
  106.5 0.9 fusion.30
  107.4 0.9 fusion.22
  108.4 0.9 fusion.14
  109.3 0.9 fusion.6
  110.3 0.9 fusion.12
  111.2 0.9 fusion.20
  112.2 0.9 fusion.28
  113.1 9.3 %all-gather.1 = f32[64,128]{1,0:T(8,128)S(1)} all-gather(f32[8,128]{1,0:T(8,128)S(1)} %add_multiply_fusion.2), channel_id=3, replica_groups=mesh['gx'=8,'pa'=4] {'gx'}, dimensions={0}, use_global_device_ids=true | all-gather | bytes 36864 | tf_op jit(solution)/shard_map/all_gather | solution.py:96
  126.4 0.9 fusion.2
  127.3 0.9 fusion.10
  128.3 0.9 fusion.18
  129.2 0.9 fusion.26
  (60 shorter events, 12.6 us)
Async XLA Ops:
  1.4 3.2 %collective-permute-start = (f32[8,128]{1,0:T(8,128)S(1)}, f32[8,128]{1,0:T(8,128)S(1)}, u32[]{:S(2)}, u32[]{:S(2)}) collective-permute-start(f32[8,128]{1,0:T(8,128)S(1)} %slice_bitcast_fusion.36), channel_id=1, source_target_pairs={{0,4},{4,8},{8,12},{12,16},{16,20},{20,24},{24,28},{1,5},{5,9},{9,... | collective-permute-start | bytes 12296 | tf_op jit(solution)/shard_map/ppermute | solution.py:26
  9.1 4.1 %collective-permute-start.1 = (f32[1,8,128,128]{3,2,1,0:T(8,128)S(1)}, f32[1,8,128,128]{3,2,1,0:T(8,128)S(1)}, u32[]{:S(2)}, u32[]{:S(2)}) collective-permute-start(f32[1,8,128,128]{3,2,1,0:T(8,128)S(1)} %convolution_bitcast_fusion), channel_id=1, source_target_pairs={{0,4},{4,0},{8,12},{12,8},{16,20},{20,16},{24,28},{28,24},{1,5},{5... | collective-permute-start | bytes 1572872 | tf_op jit(solution)/shard_map/ppermute | solution.py:12
  13.4 26.2 %collective-permute-start.2 = (f32[2,8,128,128]{3,2,1,0:T(8,128)S(1)}, f32[2,8,128,128]{3,2,1,0:T(8,128)}, u32[]{:S(2)}, u32[]{:S(2)}) collective-permute-start(f32[2,8,128,128]{3,2,1,0:T(8,128)S(1)} %maximum_select_fusion.2), channel_id=1, source_target_pairs={{0,8},{4,12},{8,0},{12,4},{16,24},{20,28},{24,16},{28,20},{1,9},{5... | collective-permute-start | bytes 3145736 | tf_op jit(solution)/shard_map/ppermute | solution.py:12
  16.0 29.3 %copy-start = (f32[4,8,128,128]{3,2,1,0:T(8,128)S(1)}, f32[4,8,128,128]{3,2,1,0:T(8,128)}, u32[]{:S(2)}) copy-start(f32[4,8,128,128]{3,2,1,0:T(8,128)} %param.6) | copy-start | bytes 6291460
  16.0 30.3 %copy-start.1 = (f32[4,8,128]{2,1,0:T(8,128)S(1)}, f32[4,8,128]{2,1,0:T(8,128)}, u32[]{:S(2)}) copy-start(f32[4,8,128]{2,1,0:T(8,128)} %param.7) | copy-start | bytes 49156
  42.6 51.5 %collective-permute-start.3 = (f32[4,8,128,128]{3,2,1,0:T(8,128)}, f32[4,8,128,128]{3,2,1,0:T(8,128)}, u32[]{:S(2)}, u32[]{:S(2)}) collective-permute-start(f32[4,8,128,128]{3,2,1,0:T(8,128)} %maximum_select_fusion.1), channel_id=1, source_target_pairs={{0,16},{4,20},{8,24},{12,28},{16,0},{20,4},{24,8},{28,12},{1,17},{... | collective-permute-start | bytes 6291464 | tf_op jit(solution)/shard_map/ppermute | solution.py:12
  124.1 6.1 %copy-start.2 = (s32[4,8,128]{2,1,0:T(8,128)S(1)}, s32[4,8,128]{2,1,0:T(8,128)}, u32[]{:S(2)}) copy-start(s32[4,8,128]{2,1,0:T(8,128)} %param.10) | copy-start | bytes 49156
